TPU v7x, 32 devices: a whole 2x2x4 slice. The times are simulated.
32 devices in a mesh: row: 4 (over z), col: 8 (over y, x, core).
Axes of the slice: x: 2, y: 2, z: 4, core: 2. Of those that a mesh axis runs over, the one named last changes fastest.
Arguments:
- pair: bfloat16 [256, 256, 128], P('row', 'col'), may hold values from -6 to 6
- residue_mask: int32 [256], replicated, may hold values 0 or 1
- norm_gain: float32 [2, 2, 128], replicated, may hold values from 0.25 to 1.75
- norm_bias: float32 [2, 2, 128], replicated, may hold values from -3 to 3
- w_in_q: bfloat16 [2, 128, 640], replicated, may hold values from -0.5 to 0.5
- exp_in: int32 [2, 4, 20], replicated, may hold values from -2 to 1
- w_out_q: bfloat16 [2, 128, 128], replicated, may hold values from -0.5 to 0.5
- exp_out: int32 [2, 4, 4], replicated, may hold values from -2 to 1
Outputs:
- pair_out: bfloat16 [256, 256, 128], P('row', 'col')
All inputs are finite; a program needn't handle non-finite values.
Results may differ from a plain program's by a relative error of at most 0.0056.
Values may be sent and summed in bfloat16 or wider, within the bound.
No kernel may reach another device: no remote copies, remote signals or barrier semaphores. Data moves between devices by JAX's collectives and lax.ppermute only.
A program may use at most 128 MiB of HBM per device.

v0:
```python
import jax
import jax.numpy as jnp
from jax import lax
from jax.sharding import PartitionSpec as P

BLK = 32


def spread(x, axis, root):
    mine = lax.axis_index(axis) == root
    return lax.psum(jnp.where(mine, x, jnp.zeros_like(x)), axis)


def layer_norm(values, scale_vec, shift_vec):
    average = jnp.mean(values, axis=-1, keepdims=True)
    centred = values - average
    variance = jnp.mean(centred * centred, axis=-1, keepdims=True)
    return centred * lax.rsqrt(variance + 1e-05) * scale_vec + shift_vec


def dequantize(quantized, exponents, block_size):
    scales = jnp.exp2(exponents.astype(jnp.float32))
    scales = jnp.repeat(jnp.repeat(scales, block_size, axis=0), block_size, axis=1)
    return (quantized.astype(jnp.float32) * scales).astype(jnp.bfloat16)


def project(pair_in, row_mask, col_mask, layer, norm_gain, norm_bias, w_in_q, exp_in):
    rows_n, cols_n, width = pair_in.shape
    normed = layer_norm(
        pair_in.astype(jnp.float32), norm_gain[layer, 0], norm_bias[layer, 0]
    ).astype(jnp.bfloat16)
    weights_in = dequantize(w_in_q[layer], exp_in[layer], BLK)
    projected = jnp.dot(
        normed.reshape(rows_n * cols_n, width), weights_in, preferred_element_type=jnp.float32
    )
    projected = projected.reshape(rows_n, cols_n, 5 * width)
    pair_mask = (row_mask[:, None] * col_mask[None, :])[:, :, None]
    left = (
        jax.nn.sigmoid(projected[:, :, 0:width]) * projected[:, :, width : 2 * width] * pair_mask
    ).astype(jnp.bfloat16)
    right = (
        jax.nn.sigmoid(projected[:, :, 2 * width : 3 * width])
        * projected[:, :, 3 * width : 4 * width]
        * pair_mask
    ).astype(jnp.bfloat16)
    gate = jax.nn.sigmoid(projected[:, :, 4 * width :])
    return (left, right, gate)


def finish(pair_in, summed, gate, layer, norm_gain, norm_bias, w_out_q, exp_out):
    rows_n, cols_n, width = pair_in.shape
    normed = layer_norm(summed, norm_gain[layer, 1], norm_bias[layer, 1]).astype(jnp.bfloat16)
    weights_out = dequantize(w_out_q[layer], exp_out[layer], BLK)
    update = jnp.dot(
        normed.reshape(rows_n * cols_n, width), weights_out, preferred_element_type=jnp.float32
    )
    update = update.reshape(rows_n, cols_n, width)
    return (pair_in.astype(jnp.float32) + gate * update).astype(jnp.bfloat16)


def shards(pair, residue_mask, norm_gain, norm_bias, w_in_q, exp_in, w_out_q, exp_out):
    rows_n, cols_n, width = pair.shape
    row_count = lax.axis_size("row")
    col_count = lax.axis_size("col")
    col_ratio = col_count // row_count
    row_place = lax.axis_index("row")
    col_place = lax.axis_index("col")
    mask_all = residue_mask.astype(jnp.float32)
    row_mask = lax.dynamic_slice_in_dim(mask_all, row_place * rows_n, rows_n)
    col_mask = lax.dynamic_slice_in_dim(mask_all, col_place * cols_n, cols_n)
    left, right, gate = project(pair, row_mask, col_mask, 0, norm_gain, norm_bias, w_in_q, exp_in)
    right_panel = lax.all_gather(right, "col", axis=1, tiled=True)
    chosen = lax.dynamic_slice_in_dim(right_panel, col_place % col_ratio * cols_n, cols_n, 0)
    right_rows = spread(chosen, "row", col_place // col_ratio)
    selected = right_rows
    summed = jnp.einsum(
        "ikc,jkc->ijc",
        lax.all_gather(left, "col", axis=1, tiled=True),
        selected,
        preferred_element_type=jnp.float32,
    )
    pair_mid = finish(pair, summed, gate, 0, norm_gain, norm_bias, w_out_q, exp_out)
    left, right, gate = project(
        pair_mid, row_mask, col_mask, 1, norm_gain, norm_bias, w_in_q, exp_in
    )
    column_panel = lax.all_gather(left, "row", axis=0, tiled=True)
    pieces_list = []
    for offset_idx in range(col_ratio):
        pieces_list.append(spread(column_panel, "col", row_place * col_ratio + offset_idx))
    left_cols = jnp.concatenate(pieces_list, axis=1)
    selected = left_cols
    summed = jnp.einsum(
        "kic,kjc->ijc",
        selected,
        lax.all_gather(right, "row", axis=0, tiled=True),
        preferred_element_type=jnp.float32,
    )
    return finish(pair_mid, summed, gate, 1, norm_gain, norm_bias, w_out_q, exp_out)


def solution(mesh):
    placed = (P("row", "col", None), P(), P(), P(), P(), P(), P(), P())
    return jax.shard_map(
        shards, mesh=mesh, in_specs=placed, out_specs=P("row", "col", None), check_vma=False
    )
```

profile of v0, /device:TPU:0, one launch (start us, length us, event | category | flops | bytes accessed | tf_op | source)
XLA Modules:
  0.0 389.6 jit_solution(5334776976437683013)
XLA Ops:
  6.5 0.7 convert_element_type.115
  7.3 0.1 dynamic_slice.10
  7.4 0.1 dynamic_slice.9
  7.4 1.0 fusion.65
  8.5 0.2 copy.126
  8.6 0.7 exponential_bitcast_fusion.1
  9.3 0.1 copy.96
  9.4 0.1 broadcast_in_dim.49
  9.5 0.1 reshape.147
  9.6 1.4 convert_reduce_fusion.1
  11.0 0.1 copy.91
  11.1 0.1 copy.92
  11.2 0.6 fusion.14
  11.8 0.1 copy.93
  11.9 0.1 copy.94
  12.0 0.1 broadcast_multiply_fusion
  12.1 1.0 fusion.44
  13.2 2.1 fusion.32
  15.2 0.6 copy-done
  15.9 0.7 all-gather.7.cloned.1.call-update
  16.7 39.4 %all-gather.5.cloned.1.call-done = bf16[64,256,128]{2,1,0:T(8,128)(2,1)} async-done(((bf16[64,32,128]{2,1,0:T(8,128)(2,1)}), bf16[64,256,128]{2,1,0:T(8,128)(2,1)}) %all-gather.5.cloned.1.call-update) | async-done | bytes 4194320 | tf_op jit(solution)/shard_map/all_gather | solution.py:72
  56.1 3.1 dynamic-slice_select_fusion
  59.3 0.8 copy-done.3
  60.0 0.1 copy.127
  60.2 0.1 copy.101
  60.3 0.1 broadcast_in_dim.53
  60.3 0.1 reshape.148
  60.4 0.2 copy.128
  60.6 0.1 copy.109
  60.7 0.1 broadcast_in_dim.56
  60.8 0.1 reshape.149
  60.9 34.4 %all-gather.7.cloned.1.call-done = bf16[64,256,128]{2,1,0:T(8,128)(2,1)} async-done(((bf16[64,32,128]{2,1,0:T(8,128)(2,1)}), bf16[64,256,128]{2,1,0:T(8,128)(2,1)}) %all-gather.7.cloned.1.call-update) | async-done | bytes 4194320 | tf_op jit(solution)/shard_map/all_gather | solution.py:78
  95.4 15.6 %copy.99 = bf16[64,256,128]{0,1,2:T(8,128)(2,1)} copy(bf16[64,256,128]{2,1,0:T(8,128)(2,1)} %all-gather.7.cloned.1.call-done) | data formatting | bytes 8388608 | tf_op jit(solution)/shard_map/all_gather | solution.py:78
  111.0 72.9 %all-reduce.4.cloned.1.call-done = bf16[32,256,128]{2,1,0:T(8,128)(2,1)} async-done(((bf16[32,256,128]{2,1,0:T(8,128)(2,1)}), bf16[32,256,128]{2,1,0:T(8,128)(2,1)}) %all-reduce.4.cloned.1.call-update) | async-done | bytes 2097168 | tf_op jit(solution)/shard_map/psum | solution.py:11
  183.9 3.4 copy.98
  187.3 4.8 %bitcast_reduce_fusion.1 = (f32[64,32]{0,1:T(8,128)S(1)}, f32[128,32,64]{2,1,0:T(8,128)S(1)}) fusion(bf16[32,256,128]{1,0,2:T(8,128)(2,1)S(1)} %copy.98, bf16[64,256,128]{0,1,2:T(8,128)(2,1)} %copy.99), kind=kOutput, calls=%fused_computation.7 | convolution fusion | flops 134477824 | bytes 7348224 | tf_op jit(solution)/shard_map/ikc,jkc->ijc/dot_general | solution.py:76
  192.1 0.3 multiply_reduce_fusion.1
  192.5 0.4 add_convert_fusion.1
  192.9 1.5 copy.102
  194.5 1.8 convert_reduce_fusion
  196.3 0.1 copy.105
  196.4 0.6 fusion.10
  197.0 0.1 copy.106
  197.1 0.1 copy.107
  197.2 1.0 fusion.46
  198.3 2.0 fusion.19
  200.2 0.7 copy-done.1
  201.0 0.5 all-gather.9.cloned.1.call-update
  201.5 0.2 all-reduce.6.cloned.1.call-start
  201.7 44.0 %all-gather.11.cloned.1.call-done = bf16[256,32,128]{2,1,0:T(8,128)(2,1)} async-done(((bf16[64,32,128]{2,1,0:T(8,128)(2,1)}), bf16[256,32,128]{2,1,0:T(8,128)(2,1)}) %all-gather.11.cloned.1.call-update) | async-done | bytes 2097168 | tf_op jit(solution)/shard_map/all_gather | solution.py:86
  245.8 3.9 %copy.111 = bf16[256,32,128]{0,1,2:T(8,128)(2,1)S(1)} copy(bf16[256,32,128]{2,1,0:T(8,128)(2,1)} %all-gather.11.cloned.1.call-done) | data formatting | bytes 4194304 | tf_op jit(solution)/shard_map/all_gather | solution.py:86
  249.7 2.3 broadcast_select_fusion.1
  252.0 0.1 copy.129
  252.1 0.1 copy.115
  252.2 0.1 broadcast_in_dim.59
  252.3 0.1 reshape.150
  252.4 39.3 %all-gather.9.cloned.1.call-done = bf16[256,32,128]{2,1,0:T(8,128)(2,1)} async-done(((bf16[64,32,128]{2,1,0:T(8,128)(2,1)}), bf16[256,32,128]{2,1,0:T(8,128)(2,1)}) %all-gather.9.cloned.1.call-update) | async-done | bytes 2097168 | tf_op jit(solution)/shard_map/all_gather | solution.py:95
  291.7 3.9 %copy.113 = bf16[256,32,128]{0,1,2:T(8,128)(2,1)S(1)} copy(bf16[256,32,128]{2,1,0:T(8,128)(2,1)} %all-gather.9.cloned.1.call-done) | data formatting | bytes 4194304 | tf_op jit(solution)/shard_map/all_gather | solution.py:95
  295.6 78.9 %all-reduce.6.cloned.1.call-done = (bf16[256,32,128]{0,1,2:T(8,128)(2,1)}, bf16[256,32,128]{0,1,2:T(8,128)(2,1)}) async-done(((bf16[256,32,128]{0,1,2:T(8,128)(2,1)}, bf16[256,32,128]{0,1,2:T(8,128)(2,1)}), (bf16[256,32,128]{0,1,2:T(8,128)(2,1)}, bf16[256,32,128]{0,1,2:T(8,128)(2,1)})) %all-reduce.6.cloned.1.call-update) | async-done | bytes 4194320 | tf_op jit(solution)/shard_map/psum | solution.py:11
  374.5 3.4 bitcast_reduce_fusion
  378.0 0.3 multiply_reduce_fusion
  378.3 0.4 add_convert_fusion
  378.7 1.5 copy.116
  380.3 2.4 fusion.5
  (36 shorter events, 0.5 us)
Async XLA Ops:
  6.5 4.6 %copy-start.2 = (bf16[64,32,128]{2,1,0:T(8,128)(2,1)S(1)}, bf16[64,32,128]{2,1,0:T(8,128)(2,1)}, u32[]{:S(2)}) copy-start(bf16[64,32,128]{2,1,0:T(8,128)(2,1)} %param.8) | copy-start | bytes 1572868
  6.5 5.5 %copy-start.6 = (f32[2,2,128]{2,1,0:T(2,128)S(1)}, f32[2,2,128]{2,1,0:T(2,128)}, u32[]{:S(2)}) copy-start(f32[2,2,128]{2,1,0:T(2,128)} %param.10) | copy-start | bytes 6148
  6.5 5.5 %copy-start.5 = (f32[2,2,128]{2,1,0:T(2,128)S(1)}, f32[2,2,128]{2,1,0:T(2,128)}, u32[]{:S(2)}) copy-start(f32[2,2,128]{2,1,0:T(2,128)} %param.11) | copy-start | bytes 6148
  6.5 49.6 %all-gather.5.cloned.1.call-start = ((), (), s32[]{:S(2)}) async-start(), calls=%async_computation | async-start | bytes 4718592 | tf_op jit(solution)/shard_map/all_gather | solution.py:72
  13.2 2.7 copy-start
  15.9 79.5 %all-gather.7.cloned.1.call-start = ((), (), s32[]{:S(2)}) async-start(), calls=%async_computation.2 | async-start | bytes 4718592 | tf_op jit(solution)/shard_map/all_gather | solution.py:78
  16.7 167.3 %all-reduce.4.cloned.1.call-start = ((), (), s32[]{:S(2)}) async-start(), calls=%async_computation.1 | async-start | bytes 4194304 | tf_op jit(solution)/shard_map/psum | solution.py:11
  59.2 0.8 copy-start.3
  59.2 1.0 copy-start.4
  59.2 186.6 %all-gather.11.cloned.1.call-start = ((), (), s32[]{:S(2)}) async-start(), calls=%async_computation.4 | async-start | bytes 2621440 | tf_op jit(solution)/shard_map/all_gather | solution.py:86
  198.2 2.6 copy-start.1
  200.9 90.8 %all-gather.9.cloned.1.call-start = ((), (), s32[]{:S(2)}) async-start(), calls=%async_computation.3 | async-start | bytes 2621440 | tf_op jit(solution)/shard_map/all_gather | solution.py:95
  201.5 173.0 %all-reduce.6.cloned.1.call-start = ((), (), s32[]{:S(2)}) async-start(), calls=%async_computation.5 | async-start | bytes 8388608 | tf_op jit(solution)/shard_map/psum | solution.py:11
Sparse Core Ops, SparseCore 0:
  16.0 40.0 all-gather.4
  58.0 37.3 all-gather.6
  97.7 86.1 all-reduce.3
  201.0 44.6 all-gather.10
  247.2 44.4 all-gather.8
  294.8 79.6 all-reduce.5
where the time goes:
time: 390 us
  waiting for transfers between devices  310 us (79%)
  local copies, waits for them, and re-layouts  35.4 us (9%)
  other arithmetic  15.3 us (4%)
  matrix products  14.5 us (4%)
  between operations  13.8 us (4%)
    psum x2, waiting for transfers between devices, spread(): return lax.psum(jnp.where(mine, x, jnp.zeros_like(x)), axis)  152 us
    all_gather x1, waiting for transfers between devices, shards(): column_panel = lax.all_gather(left, 'row', axis=0, tiled=True)  44 us
    all_gather x1, waiting for transfers between devices, shards(): right_panel = lax.all_gather(right, 'col', axis=1, tiled=True)  39.4 us
    all_gather x1, waiting for transfers between devices, shards(): lax.all_gather(right, 'row', axis=0, tiled=True)  39.3 us
    all_gather x1, waiting for transfers between devices, shards(): lax.all_gather(left, 'col', axis=1, tiled=True)  34.4 us
    all_gather x1, local copies, waits for them, and re-layouts, shards(): lax.all_gather(left, 'col', axis=1, tiled=True)  15.6 us
  transfers between devices with their start and end apart: 6, of which 6 were waited for; matrix products, arithmetic and copies ran while one was open for 8% of the time, Pallas kernels for 0%

commit v1 on v0

--- a/solution.py
+++ b/solution.py
@@ -4,6 +4,28 @@
 from jax.sharding import PartitionSpec as P
 
 BLK = 32
+
+
+def joined_along(blocks, dim):
+    shape = list(blocks.shape[1:])
+    shape[dim] *= blocks.shape[0]
+    return jnp.moveaxis(blocks, 0, dim).reshape(shape)
+
+
+def grow_blocks(x, axis):
+    peers = lax.axis_size(axis)
+    parts = x[None]
+    for level in range(peers.bit_length() - 1):
+        bit = 1 << level
+        other = lax.ppermute(parts, axis, [(i, i ^ bit) for i in range(peers)])
+        both = jnp.stack([parts, other])
+        upper = lax.axis_index(axis) >> level & 1
+        parts = jnp.where(upper == 0, both, both[::-1]).reshape(-1, *x.shape)
+    return parts
+
+
+def collect(x, axis, dim):
+    return joined_along(grow_blocks(x, axis), dim)
 
 
 def spread(x, axis, root):
@@ -90,10 +112,7 @@
     left_cols = jnp.concatenate(pieces_list, axis=1)
     selected = left_cols
     summed = jnp.einsum(
-        "kic,kjc->ijc",
-        selected,
-        lax.all_gather(right, "row", axis=0, tiled=True),
-        preferred_element_type=jnp.float32,
+        "kic,kjc->ijc", selected, collect(right, "row", 0), preferred_element_type=jnp.float32
     )
     return finish(pair_mid, summed, gate, 1, norm_gain, norm_bias, w_out_q, exp_out)
 

time: 390 us -> 351 us (0.900)
  waiting for transfers between devices: 310 us -> 265 us
    psum x2, waiting for transfers between devices: 152 us -> 98 us  [spread(): return lax.psum(jnp.where(mine, x, jnp.zeros_like(x)), axis)]
    ppermute x0 -> x2, waiting for transfers between devices: none -> 45.9 us  [grow_blocks(): other = lax.ppermute(parts, axis, [(i, i ^ bit) for i in range(peers)])]
    all_gather x1 -> x0, waiting for transfers between devices: 39.3 us -> none  [shards(): lax.all_gather(right, 'row', axis=0, tiled=True)]
    all_gather x1 -> x0, local copies, waits for them, and re-layouts: 3.91 us -> none  [shards(): lax.all_gather(right, 'row', axis=0, tiled=True)]
  transfers between devices with their start and end apart: 6 -> 7, of which waited for: 6 -> 6; matrix products, arithmetic and copies ran while one was open for 8% -> 9% of each run, Pallas kernels for 0% -> 0%
where the time goes in v1:
time: 351 us
  waiting for transfers between devices  265 us (75%)
  local copies, waits for them, and re-layouts  35 us (10%)
  other arithmetic  18.6 us (5%)
  matrix products  15.1 us (4%)
  between operations  13.5 us (4%)
    psum x2, waiting for transfers between devices, spread(): return lax.psum(jnp.where(mine, x, jnp.zeros_like(x)), axis)  98 us
    all_gather x1, waiting for transfers between devices, shards(): column_panel = lax.all_gather(left, 'row', axis=0, tiled=True)  47 us
    ppermute x2, waiting for transfers between devices, grow_blocks(): other = lax.ppermute(parts, axis, [(i, i ^ bit) for i in range(peers)])  45.9 us
    all_gather x1, waiting for transfers between devices, shards(): right_panel = lax.all_gather(right, 'col', axis=1, tiled=True)  39.4 us
    all_gather x1, waiting for transfers between devices, shards(): lax.all_gather(left, 'col', axis=1, tiled=True)  34.4 us
    all_gather x1, local copies, waits for them, and re-layouts, shards(): lax.all_gather(left, 'col', axis=1, tiled=True)  15.6 us
  transfers between devices with their start and end apart: 7, of which 6 were waited for; matrix products, arithmetic and copies ran while one was open for 9% of the time, Pallas kernels for 0%

profile of v1, /device:TPU:0, one launch (start us, length us, event | category | flops | bytes accessed | tf_op | source)
XLA Modules:
  0.0 350.6 jit_solution(12621617376877053779)
XLA Ops:
  6.5 0.7 convert_element_type.115
  7.3 0.1 dynamic_slice.10
  7.4 0.1 dynamic_slice.9
  7.4 1.0 fusion.67
  8.5 0.2 copy.126
  8.6 0.7 exponential_bitcast_fusion.1
  9.3 0.1 copy.96
  9.4 0.1 broadcast_in_dim.52
  9.5 0.1 reshape.150
  9.6 1.4 convert_reduce_fusion.1
  11.1 0.1 copy.92
  11.2 0.6 fusion.14
  11.9 0.1 copy.94
  12.0 0.1 broadcast_multiply_fusion
  12.1 1.0 fusion.46
  13.2 2.1 fusion.32
  15.3 0.6 copy-done
  15.9 0.7 all-gather.6.cloned.1.call-update
  16.7 39.4 %all-gather.4.cloned.1.call-done = bf16[64,256,128]{2,1,0:T(8,128)(2,1)} async-done(((bf16[64,32,128]{2,1,0:T(8,128)(2,1)}), bf16[64,256,128]{2,1,0:T(8,128)(2,1)}) %all-gather.4.cloned.1.call-update) | async-done | bytes 4194320 | tf_op jit(solution)/shard_map/all_gather | solution.py:94
  56.1 3.1 dynamic-slice_select_fusion
  59.2 0.8 copy-done.3
  60.0 0.1 copy.127
  60.1 0.1 copy.101
  60.3 0.1 reshape.151
  60.4 0.2 copy.128
  60.6 0.1 copy.109
  60.7 0.1 broadcast_in_dim.59
  60.8 0.1 reshape.152
  60.9 34.4 %all-gather.6.cloned.1.call-done = bf16[64,256,128]{2,1,0:T(8,128)(2,1)} async-done(((bf16[64,32,128]{2,1,0:T(8,128)(2,1)}), bf16[64,256,128]{2,1,0:T(8,128)(2,1)}) %all-gather.6.cloned.1.call-update) | async-done | bytes 4194320 | tf_op jit(solution)/shard_map/all_gather | solution.py:100
  95.4 15.6 %copy.99 = bf16[64,256,128]{0,1,2:T(8,128)(2,1)} copy(bf16[64,256,128]{2,1,0:T(8,128)(2,1)} %all-gather.6.cloned.1.call-done) | data formatting | bytes 8388608 | tf_op jit(solution)/shard_map/all_gather | solution.py:100
  111.0 72.9 %all-reduce.4.cloned.1.call-done = bf16[32,256,128]{2,1,0:T(8,128)(2,1)} async-done(((bf16[32,256,128]{2,1,0:T(8,128)(2,1)}), bf16[32,256,128]{2,1,0:T(8,128)(2,1)}) %all-reduce.4.cloned.1.call-update) | async-done | bytes 2097168 | tf_op jit(solution)/shard_map/psum | solution.py:33
  183.9 3.4 copy.98
  187.3 4.8 %bitcast_reduce_fusion.1 = (f32[64,32]{0,1:T(8,128)S(1)}, f32[128,32,64]{2,1,0:T(8,128)S(1)}) fusion(bf16[32,256,128]{1,0,2:T(8,128)(2,1)S(1)} %copy.98, bf16[64,256,128]{0,1,2:T(8,128)(2,1)} %copy.99), kind=kOutput, calls=%fused_computation.9 | convolution fusion | flops 134477824 | bytes 7348224 | tf_op jit(solution)/shard_map/ikc,jkc->ijc/dot_general | solution.py:98
  192.1 0.3 multiply_reduce_fusion.1
  192.5 0.4 add_convert_fusion.1
  192.9 1.5 copy.102
  194.4 1.8 convert_reduce_fusion
  196.3 0.1 copy.105
  196.4 0.6 fusion.10
  197.1 0.1 copy.107
  197.2 1.0 fusion.48
  198.2 1.8 fusion.19
  200.0 0.7 copy-done.1
  200.7 0.2 all-reduce.6.cloned.1.call-start
  201.0 0.5 collective-permute-start
  201.4 47.0 %all-gather.8.cloned.1.call-done = bf16[256,32,128]{2,1,0:T(8,128)(2,1)} async-done(((bf16[64,32,128]{2,1,0:T(8,128)(2,1)}), bf16[256,32,128]{2,1,0:T(8,128)(2,1)}) %all-gather.8.cloned.1.call-update) | async-done | bytes 2097168 | tf_op jit(solution)/shard_map/all_gather | solution.py:108
  248.4 3.9 %copy.111 = bf16[256,32,128]{0,1,2:T(8,128)(2,1)S(1)} copy(bf16[256,32,128]{2,1,0:T(8,128)(2,1)} %all-gather.8.cloned.1.call-done) | data formatting | bytes 4194304 | tf_op jit(solution)/shard_map/all_gather | solution.py:108
  252.4 2.3 broadcast_select_fusion.1
  254.7 1.1 pad_maximum_fusion.1
  255.9 0.4 fusion.45
  256.3 2.1 collective-permute-start.1
  258.4 0.1 copy.129
  258.5 0.1 copy.115
  258.7 0.1 reshape.154
  258.8 45.9 %collective-permute-done.1 = bf16[2,64,32,128]{3,2,1,0:T(8,128)(2,1)} collective-permute-done((bf16[2,64,32,128]{3,2,1,0:T(8,128)(2,1)S(1)}, bf16[2,64,32,128]{3,2,1,0:T(8,128)(2,1)}, u32[]{:S(2)}, u32[]{:S(2)}) %collective-permute-start.1) | collective-permute-done | bytes 1048608 | tf_op jit(solution)/shard_map/ppermute | solution.py:20
  304.7 1.4 pad_maximum_fusion
  306.1 0.5 reverse_select_fusion
  306.6 3.6 %copy.113 = bf16[256,32,128]{0,1,2:T(8,128)(2,1)} copy(bf16[256,32,128]{2,1,0:T(8,128)(2,1)S(1)} %bitcast.94) | data formatting | bytes 4194304 | tf_op jit(solution)/shard_map/reshape;reshape | solution.py:12
  310.2 25.1 %all-reduce.6.cloned.1.call-done = (bf16[256,32,128]{0,1,2:T(8,128)(2,1)}, bf16[256,32,128]{0,1,2:T(8,128)(2,1)}) async-done(((bf16[256,32,128]{0,1,2:T(8,128)(2,1)}, bf16[256,32,128]{0,1,2:T(8,128)(2,1)}), (bf16[256,32,128]{0,1,2:T(8,128)(2,1)}, bf16[256,32,128]{0,1,2:T(8,128)(2,1)})) %all-reduce.6.cloned.1.call-update) | async-done | bytes 4194320 | tf_op jit(solution)/shard_map/psum | solution.py:33
  335.2 4.1 %bitcast_reduce_fusion = (f32[64,32]{0,1:T(8,128)S(1)}, f32[128,32,64]{2,1,0:T(8,128)S(1)}) fusion(bf16[256,32,128]{0,1,2:T(8,128)(2,1)} %copy.113, bf16[256,32,128]{0,1,2:T(8,128)(2,1)} %get-tuple-element.5, bf16[256,32,128]{0,1,2:T(8,128)(2,1)} %get-tuple-element.6), kind=kOutput, calls=%fused_computation.7 | convolution fusion | flops 142866432 | bytes 7348224 | tf_op jit(solution)/shard_map/kic,kjc->ijc/dot_general | solution.py:114
  339.3 0.3 multiply_reduce_fusion
  339.6 0.4 add_convert_fusion
  340.1 1.5 copy.116
  341.6 2.4 fusion.5
  (41 shorter events, 0.8 us)
Async XLA Ops:
  6.5 4.6 %copy-start.2 = (bf16[64,32,128]{2,1,0:T(8,128)(2,1)S(1)}, bf16[64,32,128]{2,1,0:T(8,128)(2,1)}, u32[]{:S(2)}) copy-start(bf16[64,32,128]{2,1,0:T(8,128)(2,1)} %param.8) | copy-start | bytes 1572868
  6.5 5.5 %copy-start.6 = (f32[2,2,128]{2,1,0:T(2,128)S(1)}, f32[2,2,128]{2,1,0:T(2,128)}, u32[]{:S(2)}) copy-start(f32[2,2,128]{2,1,0:T(2,128)} %param.10) | copy-start | bytes 6148
  6.5 5.5 %copy-start.5 = (f32[2,2,128]{2,1,0:T(2,128)S(1)}, f32[2,2,128]{2,1,0:T(2,128)}, u32[]{:S(2)}) copy-start(f32[2,2,128]{2,1,0:T(2,128)} %param.11) | copy-start | bytes 6148
  6.5 49.6 %all-gather.4.cloned.1.call-start = ((), (), s32[]{:S(2)}) async-start(), calls=%async_computation | async-start | bytes 4718592 | tf_op jit(solution)/shard_map/all_gather | solution.py:94
  13.2 2.7 copy-start
  15.9 79.5 %all-gather.6.cloned.1.call-start = ((), (), s32[]{:S(2)}) async-start(), calls=%async_computation.2 | async-start | bytes 4718592 | tf_op jit(solution)/shard_map/all_gather | solution.py:100
  16.6 167.3 %all-reduce.4.cloned.1.call-start = ((), (), s32[]{:S(2)}) async-start(), calls=%async_computation.1 | async-start | bytes 4194304 | tf_op jit(solution)/shard_map/psum | solution.py:33
  59.2 0.8 copy-start.3
  59.2 1.0 copy-start.4
  59.2 189.2 %all-gather.8.cloned.1.call-start = ((), (), s32[]{:S(2)}) async-start(), calls=%async_computation.3 | async-start | bytes 2621440 | tf_op jit(solution)/shard_map/all_gather | solution.py:108
  198.2 2.5 copy-start.1
  200.7 134.5 %all-reduce.6.cloned.1.call-start = ((), (), s32[]{:S(2)}) async-start(), calls=%async_computation.4 | async-start | bytes 8388608 | tf_op jit(solution)/shard_map/psum | solution.py:33
  201.0 53.8 %collective-permute-start = (bf16[1,64,32,128]{3,2,1,0:T(8,128)(2,1)S(1)}, bf16[1,64,32,128]{3,2,1,0:T(8,128)(2,1)}, u32[]{:S(2)}, u32[]{:S(2)}) collective-permute-start(bf16[1,64,32,128]{3,2,1,0:T(8,128)(2,1)S(1)} %bitcast.95), channel_id=1, source_target_pairs={{0,8},{8,0},{16,24},{24,16},{1,9},{9,1},{17,25},{25,17},{2,10},{10... | collective-permute-start | bytes 1572872 | tf_op jit(solution)/shard_map/ppermute | solution.py:20
  256.3 48.4 %collective-permute-start.1 = (bf16[2,64,32,128]{3,2,1,0:T(8,128)(2,1)S(1)}, bf16[2,64,32,128]{3,2,1,0:T(8,128)(2,1)}, u32[]{:S(2)}, u32[]{:S(2)}) collective-permute-start(bf16[2,64,32,128]{3,2,1,0:T(8,128)(2,1)S(1)} %get-tuple-element.14), channel_id=1, source_target_pairs={{0,16},{8,24},{16,0},{24,8},{1,17},{9,25},{17,1},{25,9},{2,18},{10... | collective-permute-start | bytes 3145736 | tf_op jit(solution)/shard_map/ppermute | solution.py:20
Sparse Core Ops, SparseCore 0:
  16.0 40.0 all-gather.3
  58.0 37.3 all-gather.5
  97.7 86.1 all-reduce.3
  200.9 47.5 all-gather.7
  254.8 80.3 all-reduce.5
